TPU v7x, 32 devices: a whole 2x2x4 slice. The times are simulated.
32 devices in a mesh: section: 4 (over y, core), shard: 2 (over x), tensor: 4 (over z).
Axes of the slice: x: 2, y: 2, z: 4, core: 2. Of those that a mesh axis runs over, the one named last changes fastest.
Arguments:
- gradient: bfloat16 [48, 2560, 1024], P('section', ('shard', 'tensor')), may hold values from -15000 to 15000
- momentum: float32 [48, 2560, 1024], P('section', ('shard', 'tensor')), may hold values from -28000 to 28000
- weight: bfloat16 [48, 2560, 1024], P('section', ('shard', 'tensor')), may hold values from -0.1875 to 0.1875
Outputs:
- new_weight: bfloat16 [48, 2560, 1024], P('section', ('shard', 'tensor'))
- new_momentum: float32 [48, 2560, 1024], P('section', ('shard', 'tensor'))
- update: bfloat16 [48, 2560, 1024], P('section', ('shard', 'tensor'))
All inputs are finite; a program needn't handle non-finite values.
Results may differ from a plain program's by a relative error of at most 0.029.
Values may be sent and summed in bfloat16 or wider, within the bound.
A program may use at most 256 MiB of HBM per device.

v0:
```python
import math
import jax
import jax.numpy as jnp
from jax import lax
from jax.sharding import PartitionSpec as P

D = 1024
HID = 2560
ITERS = 3
decay_rate = 0.95
epsilon = 1e-07
coeff_one = 3.4445
coeff_two = -4.775
coeff_three = 2.0315
learn_rate = 0.02
weight_decay = 0.1


def shortened(x):

    def short(part):
        return part.astype(jnp.bfloat16) if part.dtype == jnp.float32 else part

    return jax.tree.map(short, x)


def gram_matrix(partial_value):
    return lax.psum(partial_value.astype(jnp.bfloat16), "tensor").astype(jnp.float32)


def orthogonalize(nesterov):
    values = nesterov.astype(jnp.float32)
    total = lax.psum(jnp.sum(values * values, axis=(1, 2)), "tensor")
    current = (values / (jnp.sqrt(total)[:, None, None] + epsilon)).astype(jnp.bfloat16)
    for iteration in range(ITERS):
        partial_value = jnp.einsum(
            "krd,kre->kde", current, current, preferred_element_type=jnp.float32
        )
        gram = gram_matrix(partial_value)
        gram_bf = gram.astype(jnp.bfloat16)
        squared = jnp.einsum("kde,kef->kdf", gram_bf, gram_bf, preferred_element_type=jnp.float32)
        mixer = (coeff_two * gram + coeff_three * squared).astype(jnp.bfloat16)
        mixed = jnp.einsum("krd,kde->kre", current, mixer, preferred_element_type=jnp.float32)
        current = (coeff_one * current.astype(jnp.float32) + mixed).astype(jnp.bfloat16)
    update_gain = 0.2 * math.sqrt(max(HID, D))
    return (update_gain * current.astype(jnp.float32)).astype(jnp.bfloat16)


def apply_update(weight, update):
    weight_values = weight.astype(jnp.float32)
    return (
        weight_values - learn_rate * (update.astype(jnp.float32) + weight_decay * weight_values)
    ).astype(jnp.bfloat16)


def pad_slots(values, padded_count):
    extra = padded_count - values.shape[0]
    if extra == 0:
        return values
    filler = jnp.zeros((extra,) + values.shape[1:], values.dtype)
    return jnp.concatenate([values, filler], axis=0)


def local(gradient, momentum, weight):
    section_mats = gradient.shape[0]
    shards = lax.axis_size("shard")
    slot_count = (section_mats + shards - 1) // shards
    padded_count = slot_count * shards
    grad_dealt, weight_dealt = (
        lax.all_to_all(
            pad_slots(gradient, padded_count), "shard", split_axis=0, concat_axis=1, tiled=True
        ),
        lax.all_to_all(
            pad_slots(weight, padded_count), "shard", split_axis=0, concat_axis=1, tiled=True
        ),
    )
    moment_dealt = lax.all_to_all(
        pad_slots(momentum, padded_count).astype(jnp.bfloat16),
        "shard",
        split_axis=0,
        concat_axis=1,
        tiled=True,
    ).astype(jnp.float32)
    grad_values = grad_dealt.astype(jnp.float32)
    new_momentum = decay_rate * moment_dealt + grad_values
    nesterov = (grad_values + decay_rate * new_momentum).astype(jnp.bfloat16)
    update = orthogonalize(nesterov)
    new_weight = apply_update(weight_dealt, update)
    back_weight, back_update = (
        lax.all_to_all(new_weight, "shard", split_axis=1, concat_axis=0, tiled=True),
        lax.all_to_all(update, "shard", split_axis=1, concat_axis=0, tiled=True),
    )
    back_moment = lax.all_to_all(
        shortened(new_momentum), "shard", split_axis=1, concat_axis=0, tiled=True
    ).astype(new_momentum.dtype)
    return (back_weight[:section_mats], back_moment[:section_mats], back_update[:section_mats])


def solution(mesh):
    return jax.shard_map(
        local,
        mesh=mesh,
        in_specs=(
            P("section", ("shard", "tensor"), None),
            P("section", ("shard", "tensor"), None),
            P("section", ("shard", "tensor"), None),
        ),
        out_specs=(
            P("section", ("shard", "tensor"), None),
            P("section", ("shard", "tensor"), None),
            P("section", ("shard", "tensor"), None),
        ),
        check_vma=False,
    )
```

profile of v0, /device:TPU:0, one launch (start us, length us, event | category | flops | bytes accessed | tf_op | source)
XLA Modules:
  0.0 1968.1 jit_solution(14599514388412769811)
XLA Ops:
  17.1 98.9 %all_to_all.72 = bf16[12,320,1024]{2,1,0:T(8,128)(2,1)} all-to-all(bf16[12,320,1024]{2,1,0:T(8,128)(2,1)} %convert_element_type.139), channel_id=1, replica_groups=mesh['section'=4,'shard'=2,'tensor'=4] {'shard'}, dimensions={0} | all-to-all | bytes 15728640 | tf_op jit(solution)/shard_map/all_to_all | solution.py:77
  134.2 14.5 copy.17
  148.6 60.6 %all-to-all-done.1 = bf16[12,320,1024]{2,1,0:T(8,128)(2,1)} async-done(((bf16[12,320,1024]{2,1,0:T(8,128)(2,1)}), bf16[12,320,1024]{2,1,0:T(8,128)(2,1)}, u32[]{:S(2)}, u32[]{:S(2)}) %all-to-all-start.1) | async-done | bytes 7864352 | tf_op jit(solution)/shard_map/all_to_all | solution.py:70
  229.5 12.1 psum.28
  241.6 16.3 fusion.22
  257.9 17.3 convolution_convert_fusion.2
  275.8 423.0 %all-reduce.4.cloned.1.call-done = bf16[6,1024,1024]{2,1,0:T(8,128)(2,1)} async-done(((bf16[6,1024,1024]{2,1,0:T(8,128)(2,1)}), bf16[6,1024,1024]{2,1,0:T(8,128)(2,1)}) %all-reduce.4.cloned.1.call-update) | async-done | bytes 12582928 | tf_op jit(solution)/shard_map/psum | solution.py:28
  698.8 35.4 %add_convert_fusion.5 = bf16[6,640,1024]{2,1,0:T(8,128)(2,1)} fusion(bf16[6,640,1024]{2,1,0:T(8,128)(2,1)} %get-tuple-element.4, bf16[6,1024,1024]{2,1,0:T(8,128)(2,1)} %all-reduce.4.cloned.1.call-done), kind=kOutput, calls=%fused_computation.19 | convolution fusion | flops 20985151488 | bytes 28311552 | tf_op jit(solution)/shard_map/krd,kde->kre/dot_general | solution.py:43
  734.2 17.3 convolution_convert_fusion.1
  751.7 425.0 %all-reduce.6.cloned.1.call-done = bf16[6,1024,1024]{2,1,0:T(8,128)(2,1)} async-done(((bf16[6,1024,1024]{2,1,0:T(8,128)(2,1)}), bf16[6,1024,1024]{2,1,0:T(8,128)(2,1)}) %all-reduce.6.cloned.1.call-update) | async-done | bytes 12582928 | tf_op jit(solution)/shard_map/psum | solution.py:28
  1176.7 35.2 %add_convert_fusion.4 = bf16[6,640,1024]{2,1,0:T(8,128)(2,1)} fusion(bf16[6,640,1024]{2,1,0:T(8,128)(2,1)} %add_convert_fusion.5, bf16[6,1024,1024]{2,1,0:T(8,128)(2,1)} %all-reduce.6.cloned.1.call-done), kind=kOutput, calls=%fused_computation.18 | convolution fusion | flops 20985151488 | bytes 28311552 | tf_op jit(solution)/shard_map/krd,kde->kre/dot_general | solution.py:43
  1211.9 17.2 convolution_convert_fusion
  1229.1 91.7 %all_to_all.73 = bf16[12,320,1024]{2,1,0:T(8,128)(2,1)S(1)} all-to-all(bf16[12,320,1024]{2,1,0:T(8,128)(2,1)} %param.5), channel_id=1, replica_groups=mesh['section'=4,'shard'=2,'tensor'=4] {'shard'}, dimensions={0} | all-to-all | bytes 15728640 | tf_op jit(solution)/shard_map/all_to_all | solution.py:73
  1328.6 12.0 copy.23
  1348.7 305.6 %all-reduce.8.cloned.1.call-done = bf16[6,1024,1024]{2,1,0:T(8,128)(2,1)} async-done(((bf16[6,1024,1024]{2,1,0:T(8,128)(2,1)}), bf16[6,1024,1024]{2,1,0:T(8,128)(2,1)}) %all-reduce.8.cloned.1.call-update) | async-done | bytes 12582928 | tf_op jit(solution)/shard_map/psum | solution.py:28
  1654.3 38.6 %fusion.2 = (bf16[6,640,1024]{2,1,0:T(8,128)(2,1)}, bf16[6,640,1024]{2,1,0:T(8,128)(2,1)}) fusion(f32[2,6,320,1024]{3,2,0,1:T(8,128)} %copy.15, bf16[6,640,1024]{2,1,0:T(8,128)(2,1)} %add_convert_fusion.4, bf16[6,1024,1024]{2,1,0:T(8,128)(2,1)} %all-reduce.8.cloned.1.call-done), kind=kOutput, calls=%fused_computation.9 | convolution fusion | flops 21020540928 | bytes 51904512 | tf_op jit(solution)/shard_map/krd,kde->kre/dot_general | solution.py:43
  1692.9 12.0 copy.21
  1712.8 11.8 copy.25
  1724.7 103.2 %all-to-all-done.3 = bf16[6,640,1024]{2,0,1:T(8,128)(2,1)} async-done(((bf16[6,640,1024]{2,0,1:T(8,128)(2,1)}), bf16[6,640,1024]{2,0,1:T(8,128)(2,1)}, u32[]{:S(2)}, u32[]{:S(2)}) %all-to-all-start.3) | async-done | bytes 7864352 | tf_op jit(solution)/shard_map/all_to_all | solution.py:90
  1835.6 13.9 convert_bitcast_fusion
  1849.4 17.9 copy.24
  1867.3 11.6 copy.22
  1878.9 70.9 %all-to-all-done.5 = bf16[6,640,1024]{2,0,1:T(8,128)(2,1)} async-done(((bf16[6,640,1024]{2,0,1:T(8,128)(2,1)}), bf16[6,640,1024]{2,0,1:T(8,128)(2,1)}, u32[]{:S(2)}, u32[]{:S(2)}) %all-to-all-start.5) | async-done | bytes 7864352 | tf_op jit(solution)/shard_map/all_to_all | solution.py:91
  1949.8 11.6 copy.26
  (17 shorter events, 80.6 us)
Async XLA Ops:
  116.0 93.2 %all-to-all-start.1 = ((bf16[12,320,1024]{2,1,0:T(8,128)(2,1)}), bf16[12,320,1024]{2,1,0:T(8,128)(2,1)}, u32[]{:S(2)}, u32[]{:S(2)}) async-start(bf16[12,320,1024]{2,1,0:T(8,128)(2,1)} %param.3), calls=%async_computation.1 | async-start | bytes 15728640 | tf_op jit(solution)/shard_map/all_to_all | solution.py:70
  122.8 576.0 %all-reduce.4.cloned.1.call-start = ((), (), s32[]{:S(2)}) async-start(), calls=%async_computation.6 | async-start | bytes 25165824 | tf_op jit(solution)/shard_map/psum | solution.py:28
  275.2 901.5 %all-reduce.6.cloned.1.call-start = ((), (), s32[]{:S(2)}) async-start(), calls=%async_computation.7 | async-start | bytes 25165824 | tf_op jit(solution)/shard_map/psum | solution.py:28
  751.5 902.8 %all-reduce.8.cloned.1.call-start = ((), (), s32[]{:S(2)}) async-start(), calls=%async_computation.8 | async-start | bytes 25165824 | tf_op jit(solution)/shard_map/psum | solution.py:28
  1340.6 364.3 %all-to-all-start.4 = ((bf16[6,640,1024]{2,0,1:T(8,128)(2,1)}), bf16[6,640,1024]{2,0,1:T(8,128)(2,1)}, u32[]{:S(2)}, u32[]{:S(2)}) async-start(bf16[6,640,1024]{2,0,1:T(8,128)(2,1)} %copy.23), calls=%async_computation.4 | async-start | bytes 20971520 | tf_op jit(solution)/shard_map/all_to_all | solution.py:93
  1704.9 123.0 %all-to-all-start.3 = ((bf16[6,640,1024]{2,0,1:T(8,128)(2,1)}), bf16[6,640,1024]{2,0,1:T(8,128)(2,1)}, u32[]{:S(2)}, u32[]{:S(2)}) async-start(bf16[6,640,1024]{2,0,1:T(8,128)(2,1)} %copy.21), calls=%async_computation.3 | async-start | bytes 20971520 | tf_op jit(solution)/shard_map/all_to_all | solution.py:90
  1827.9 121.9 %all-to-all-start.5 = ((bf16[6,640,1024]{2,0,1:T(8,128)(2,1)}), bf16[6,640,1024]{2,0,1:T(8,128)(2,1)}, u32[]{:S(2)}, u32[]{:S(2)}) async-start(bf16[6,640,1024]{2,0,1:T(8,128)(2,1)} %copy.25), calls=%async_computation.5 | async-start | bytes 20971520 | tf_op jit(solution)/shard_map/all_to_all | solution.py:91
Sparse Core Ops, SparseCore 0:
  275.3 423.3 all-reduce.3
  751.6 425.0 all-reduce.5
  1229.2 425.0 all-reduce.7
where the time goes:
time: 1980 us; the launch traced here: 1970 us
  waiting for transfers between devices  1390 us (70%)
  blocking collectives  203 us (10%)
  matrix products  161 us (8%)
  local copies, waits for them, and re-layouts  110 us (6%)
  other arithmetic  60.6 us (3%)
  starting transfers between devices  31.2 us (2%)
    psum x3, waiting for transfers between devices, gram_matrix(): lax.psum(partial_value.astype(jnp.bfloat16), 'tensor').astype(jnp.float32)  1150 us
    dot_general x3, matrix products, orthogonalize(): jnp.einsum('krd,kde->kre', current, mixer, preferred_element_type=jnp.flo...  109 us
    all_to_all x1, waiting for transfers between devices, local(): lax.all_to_all(new_weight, 'shard', split_axis=1, concat_axis=0, tiled=True)  103 us
    all_to_all x1, blocking collectives, local(): lax.all_to_all(pad_slots(momentum, padded_count).astype(jnp.bfloat16), 's...  98.9 us
    all_to_all x1, blocking collectives, local(): lax.all_to_all(pad_slots(weight, padded_count), 'shard', split_axis=0, co...  91.7 us
    all_to_all x1, waiting for transfers between devices, local(): lax.all_to_all(update, 'shard', split_axis=1, concat_axis=0, tiled=True)  70.9 us
    all_to_all x1, waiting for transfers between devices, local(): lax.all_to_all(pad_slots(gradient, padded_count), 'shard', split_axis=0,...  60.6 us
    dot_general x3, matrix products, orthogonalize(): jnp.einsum('krd,kre->kde', current, current, preferred_element_type=jnp.f...  51.8 us
  transfers between devices with their start and end apart: 7, of which 6 were waited for; matrix products, arithmetic and copies ran while one was open for 8% of the time, Pallas kernels for 0%

commit v1 on v0

--- a/solution.py
+++ b/solution.py
@@ -25,7 +25,9 @@
 
 
 def gram_matrix(partial_value):
-    return lax.psum(partial_value.astype(jnp.bfloat16), "tensor").astype(jnp.float32)
+    return jnp.sum(lax.all_gather(partial_value.astype(jnp.bfloat16), "tensor"), axis=0).astype(
+        jnp.float32
+    )
 
 
 def orthogonalize(nesterov):

time: 1980 us -> 3280 us (1.66)
  waiting for transfers between devices: 1390 us -> 2620 us
  other arithmetic: 60.6 us -> 132 us
    all_gather x0 -> x3, waiting for transfers between devices: none -> 2380 us  [gram_matrix(): lax.all_gather(partial_value.astype(jnp.bfloat16), 'tensor')]
    psum x3 -> x0, waiting for transfers between devices: 1150 us -> none  [gram_matrix(): lax.psum(partial_value.astype(jnp.bfloat16), 'tensor').astype(jnp.float32)]
    reduce_sum x0 -> x3, other arithmetic: none -> 71.6 us  [gram_matrix(): jnp.sum(lax.all_gather(partial_value.astype(jnp.bfloat16), 'tensor'), axi...]
  transfers between devices with their start and end apart: 7 -> 7, of which waited for: 6 -> 6; matrix products, arithmetic and copies ran while one was open for 8% -> 5% of each run, Pallas kernels for 0% -> 0%
where the time goes in v1:
time: 3280 us; the launch traced here: 3270 us
  waiting for transfers between devices  2620 us (80%)
  blocking collectives  203 us (6%)
  matrix products  162 us (5%)
  other arithmetic  132 us (4%)
  local copies, waits for them, and re-layouts  110 us (3%)
    all_gather x3, waiting for transfers between devices, gram_matrix(): lax.all_gather(partial_value.astype(jnp.bfloat16), 'tensor')  2380 us
    dot_general x3, matrix products, orthogonalize(): jnp.einsum('krd,kde->kre', current, mixer, preferred_element_type=jnp.flo...  109 us
    all_to_all x1, waiting for transfers between devices, local(): lax.all_to_all(new_weight, 'shard', split_axis=1, concat_axis=0, tiled=True)  104 us
    all_to_all x1, blocking collectives, local(): lax.all_to_all(pad_slots(momentum, padded_count).astype(jnp.bfloat16), 's...  98.9 us
    all_to_all x1, blocking collectives, local(): lax.all_to_all(pad_slots(weight, padded_count), 'shard', split_axis=0, co...  91.9 us
    reduce_sum x3, other arithmetic, gram_matrix(): jnp.sum(lax.all_gather(partial_value.astype(jnp.bfloat16), 'tensor'), axi...  71.6 us
    all_to_all x1, waiting for transfers between devices, local(): lax.all_to_all(update, 'shard', split_axis=1, concat_axis=0, tiled=True)  71.1 us
  transfers between devices with their start and end apart: 7, of which 6 were waited for; matrix products, arithmetic and copies ran while one was open for 5% of the time, Pallas kernels for 0%

profile of v1, /device:TPU:0, one launch (start us, length us, event | category | flops | bytes accessed | tf_op | source)
XLA Modules:
  0.0 3269.4 jit_solution(15132391458741290272)
XLA Ops:
  17.1 98.9 %all_to_all.72 = bf16[12,320,1024]{2,1,0:T(8,128)(2,1)} all-to-all(bf16[12,320,1024]{2,1,0:T(8,128)(2,1)} %convert_element_type.145), channel_id=1, replica_groups=mesh['section'=4,'shard'=2,'tensor'=4] {'shard'}, dimensions={0} | all-to-all | bytes 15728640 | tf_op jit(solution)/shard_map/all_to_all | solution.py:79
  134.2 14.5 copy.17
  148.7 60.5 %all-to-all-done.1 = bf16[12,320,1024]{2,1,0:T(8,128)(2,1)} async-done(((bf16[12,320,1024]{2,1,0:T(8,128)(2,1)}), bf16[12,320,1024]{2,1,0:T(8,128)(2,1)}, u32[]{:S(2)}, u32[]{:S(2)}) %all-to-all-start.1) | async-done | bytes 7864352 | tf_op jit(solution)/shard_map/all_to_all | solution.py:72
  229.5 12.0 psum.7
  241.5 16.3 fusion.22
  257.8 17.6 convolution_convert_fusion.2
  275.5 833.4 %all-gather.7.cloned.1.call-done = bf16[24,1024,1024]{2,1,0:T(8,128)(2,1)} async-done(((bf16[6,1024,1024]{2,1,0:T(8,128)(2,1)}), bf16[24,1024,1024]{2,1,0:T(8,128)(2,1)}) %all-gather.7.cloned.1.call-update) | async-done | bytes 50331664 | tf_op jit(solution)/shard_map/all_gather | solution.py:28
  1108.9 23.9 reduce_sum.46
  1132.8 35.5 %add_convert_fusion.5 = bf16[6,640,1024]{2,1,0:T(8,128)(2,1)} fusion(bf16[6,640,1024]{2,1,0:T(8,128)(2,1)} %get-tuple-element.4, bf16[6,1024,1024]{2,1,0:T(8,128)(2,1)} %reduce_sum.46), kind=kOutput, calls=%fused_computation.19 | convolution fusion | flops 20985151488 | bytes 28311552 | tf_op jit(solution)/shard_map/krd,kde->kre/dot_general | solution.py:45
  1168.3 17.3 convolution_convert_fusion.1
  1185.6 834.3 %all-gather.9.cloned.1.call-done = bf16[24,1024,1024]{2,1,0:T(8,128)(2,1)} async-done(((bf16[6,1024,1024]{2,1,0:T(8,128)(2,1)}), bf16[24,1024,1024]{2,1,0:T(8,128)(2,1)}) %all-gather.9.cloned.1.call-update) | async-done | bytes 50331664 | tf_op jit(solution)/shard_map/all_gather | solution.py:28
  2019.9 24.1 reduce_sum.47
  2044.0 35.3 %add_convert_fusion.4 = bf16[6,640,1024]{2,1,0:T(8,128)(2,1)} fusion(bf16[6,640,1024]{2,1,0:T(8,128)(2,1)} %add_convert_fusion.5, bf16[6,1024,1024]{2,1,0:T(8,128)(2,1)} %reduce_sum.47), kind=kOutput, calls=%fused_computation.18 | convolution fusion | flops 20985151488 | bytes 28311552 | tf_op jit(solution)/shard_map/krd,kde->kre/dot_general | solution.py:45
  2079.4 17.5 convolution_convert_fusion
  2096.9 91.9 %all_to_all.73 = bf16[12,320,1024]{2,1,0:T(8,128)(2,1)S(1)} all-to-all(bf16[12,320,1024]{2,1,0:T(8,128)(2,1)} %param.5), channel_id=1, replica_groups=mesh['section'=4,'shard'=2,'tensor'=4] {'shard'}, dimensions={0} | all-to-all | bytes 15728640 | tf_op jit(solution)/shard_map/all_to_all | solution.py:75
  2196.6 11.9 copy.23
  2216.2 715.1 %all-gather.11.cloned.1.call-done = bf16[24,1024,1024]{2,1,0:T(8,128)(2,1)} async-done(((bf16[6,1024,1024]{2,1,0:T(8,128)(2,1)}), bf16[24,1024,1024]{2,1,0:T(8,128)(2,1)}) %all-gather.11.cloned.1.call-update) | async-done | bytes 50331664 | tf_op jit(solution)/shard_map/all_gather | solution.py:28
  2931.3 23.6 reduce_sum.48
  2954.9 38.7 %fusion.2 = (bf16[6,640,1024]{2,1,0:T(8,128)(2,1)}, bf16[6,640,1024]{2,1,0:T(8,128)(2,1)}) fusion(f32[2,6,320,1024]{3,2,0,1:T(8,128)} %copy.15, bf16[6,640,1024]{2,1,0:T(8,128)(2,1)} %add_convert_fusion.4, bf16[6,1024,1024]{2,1,0:T(8,128)(2,1)} %reduce_sum.48), kind=kOutput, calls=%fused_computation.9 | convolution fusion | flops 21020540928 | bytes 51904512 | tf_op jit(solution)/shard_map/krd,kde->kre/dot_general | solution.py:45
  2993.5 12.0 copy.21
  3025.3 103.6 %all-to-all-done.3 = bf16[6,640,1024]{2,0,1:T(8,128)(2,1)} async-done(((bf16[6,640,1024]{2,0,1:T(8,128)(2,1)}), bf16[6,640,1024]{2,0,1:T(8,128)(2,1)}, u32[]{:S(2)}, u32[]{:S(2)}) %all-to-all-start.3) | async-done | bytes 7864352 | tf_op jit(solution)/shard_map/all_to_all | solution.py:92
  3136.6 13.9 convert_bitcast_fusion
  3150.5 17.8 copy.24
  3179.9 71.1 %all-to-all-done.5 = bf16[6,640,1024]{2,0,1:T(8,128)(2,1)} async-done(((bf16[6,640,1024]{2,0,1:T(8,128)(2,1)}), bf16[6,640,1024]{2,0,1:T(8,128)(2,1)}, u32[]{:S(2)}, u32[]{:S(2)}) %all-to-all-start.5) | async-done | bytes 7864352 | tf_op jit(solution)/shard_map/all_to_all | solution.py:93
  (20 shorter events, 114.7 us)
Async XLA Ops:
  116.0 93.2 %all-to-all-start.1 = ((bf16[12,320,1024]{2,1,0:T(8,128)(2,1)}), bf16[12,320,1024]{2,1,0:T(8,128)(2,1)}, u32[]{:S(2)}, u32[]{:S(2)}) async-start(bf16[12,320,1024]{2,1,0:T(8,128)(2,1)} %param.3), calls=%async_computation.1 | async-start | bytes 15728640 | tf_op jit(solution)/shard_map/all_to_all | solution.py:72
  122.8 986.1 %all-gather.7.cloned.1.call-start = ((), (), s32[]{:S(2)}) async-start(), calls=%async_computation.6 | async-start | bytes 62914560 | tf_op jit(solution)/shard_map/all_gather | solution.py:28
  275.4 1744.5 %all-gather.9.cloned.1.call-start = ((), (), s32[]{:S(2)}) async-start(), calls=%async_computation.7 | async-start | bytes 62914560 | tf_op jit(solution)/shard_map/all_gather | solution.py:28
  1185.6 1745.7 %all-gather.11.cloned.1.call-start = ((), (), s32[]{:S(2)}) async-start(), calls=%async_computation.8 | async-start | bytes 62914560 | tf_op jit(solution)/shard_map/all_gather | solution.py:28
  2208.5 797.0 %all-to-all-start.4 = ((bf16[6,640,1024]{2,0,1:T(8,128)(2,1)}), bf16[6,640,1024]{2,0,1:T(8,128)(2,1)}, u32[]{:S(2)}, u32[]{:S(2)}) async-start(bf16[6,640,1024]{2,0,1:T(8,128)(2,1)} %copy.23), calls=%async_computation.4 | async-start | bytes 20971520 | tf_op jit(solution)/shard_map/all_to_all | solution.py:95
  3005.5 123.4 %all-to-all-start.3 = ((bf16[6,640,1024]{2,0,1:T(8,128)(2,1)}), bf16[6,640,1024]{2,0,1:T(8,128)(2,1)}, u32[]{:S(2)}, u32[]{:S(2)}) async-start(bf16[6,640,1024]{2,0,1:T(8,128)(2,1)} %copy.21), calls=%async_computation.3 | async-start | bytes 20971520 | tf_op jit(solution)/shard_map/all_to_all | solution.py:92
  3128.9 122.2 %all-to-all-start.5 = ((bf16[6,640,1024]{2,0,1:T(8,128)(2,1)}), bf16[6,640,1024]{2,0,1:T(8,128)(2,1)}, u32[]{:S(2)}, u32[]{:S(2)}) async-start(bf16[6,640,1024]{2,0,1:T(8,128)(2,1)} %copy.25), calls=%async_computation.5 | async-start | bytes 20971520 | tf_op jit(solution)/shard_map/all_to_all | solution.py:93
Sparse Core Ops, SparseCore 0:
  275.5 833.2 all-gather.6
  1185.7 834.1 all-gather.8
  2097.0 834.1 all-gather.10
